TPU v7x, 32 devices: a whole 2x2x4 slice. The times are simulated.
32 devices in a mesh: seg: 8 (over z, x), grp: 4 (over y, core).
Axes of the slice: x: 2, y: 2, z: 4, core: 2. Of those that a mesh axis runs over, the one named last changes fastest.
Arguments:
- initial_state: float32 [512], replicated, may hold values from -6 to 6
- transition: float32 [512, 512], replicated, as said below
- gains: float32 [512], replicated, may hold values from 0 to 1, as said below
- tiles: float32 [4, 4096, 512], P('grp', 'seg'), may hold values from -16 to 16
- tile_owner: int32 [4, 4096, 1], P('grp', 'seg'), may hold values from 0 to 31; in each aligned block of 512 rows (0 to 511, 512 to 1023, ..., all dimensions but the last counted through in order) at most 40 rows name the same one
- tile_step: int32 [4, 4096], P('grp', 'seg'), may hold values from 0 to 31
Outputs:
- states: float32 [4, 256, 512], P('grp', 'seg')
Inputs may be any that keep to these rules, and one draw needn't show every extreme that they name: `tile_owner`: among the tiles of one device no owner is named more than 40 times, and in some devices one owner is named exactly 40 times. `transition`: diagonal entries lie strictly between 0 and 1. `gains`: every gain is positive.
All inputs are finite; a program needn't handle non-finite values.
Results may differ from a plain program's by a relative error of at most 0.0003.
Values sent between devices are 32-bit elements; how exact they have to be, the bound alone decides.
A program may use at most 192 MiB of HBM per device.

v0:
```python
import jax
import jax.numpy as jnp
from jax import lax
from jax.sharding import PartitionSpec as P

STEP_DEV = 32


FULL = lax.Precision.HIGHEST


def carried_in(value, axis, join, neutral):
    count, mine = (lax.axis_size(axis), lax.axis_index(axis))
    pieces = jax.tree.map(lambda part: lax.all_gather(part, axis), value)
    total = jax.tree.map(
        lambda part, zero: jnp.full_like(part, 0) + jnp.asarray(zero, part.dtype), value, neutral
    )

    def lap(position, total):
        longer = join(total, jax.tree.map(lambda part: part[position], pieces))
        return jax.tree.map(lambda new, old: jnp.where(position < mine, new, old), longer, total)

    return lax.fori_loop(0, count - 1, lap, total)


def spread(block, axis, owner):
    block = jnp.where(lax.axis_index(axis) == owner, block, jnp.zeros_like(block))
    return lax.psum(block, axis)


def compose(earlier, later):
    first_map, first_shift = earlier
    second_map, second_shift = later
    joined_map = jnp.dot(second_map, first_map, precision=FULL)
    joined_shift = jnp.dot(second_map, first_shift, precision=FULL) + second_shift
    return (joined_map, joined_shift)


def on_device(initial_state, transition, gains, tiles, tile_owner, tile_step):
    width = transition.shape[0]
    n_seg = lax.axis_size("seg")
    n_grp = lax.axis_size("grp")
    n_dev = n_seg * n_grp
    tile_rows = tiles[0]
    tile_count = tile_rows.shape[0]
    capacity = max(2, 5 * tile_count // (2 * n_dev))
    owners = tile_owner[0, :, 0]
    target = owners % n_seg * n_grp + owners // n_seg
    onehot = (target[:, None] == jnp.arange(n_dev, dtype=jnp.int32)[None, :]).astype(jnp.float32)
    order = jnp.arange(tile_count, dtype=jnp.int32)
    earlier_rows = (order[:, None] > order[None, :]).astype(jnp.float32)
    before = jnp.dot(earlier_rows, onehot, precision=FULL)
    rank = jnp.sum(before * onehot, axis=1).astype(jnp.int32)
    slot_index = target * capacity + rank
    slot_total = n_dev * capacity
    buffer = jnp.zeros((slot_total, width), jnp.float32).at[slot_index].set(tile_rows)
    labels = (
        jnp.full((slot_total,), -1.0, jnp.float32)
        .at[slot_index]
        .set(tile_step[0].astype(jnp.float32))
    )
    received, marks = (
        lax.all_to_all(buffer, ("seg", "grp"), split_axis=0, concat_axis=0, tiled=True),
        lax.all_to_all(labels, ("seg", "grp"), split_axis=0, concat_axis=0, tiled=True),
    )
    step_ids = jnp.arange(STEP_DEV, dtype=jnp.float32)
    placed = (step_ids[:, None] == marks[None, :]).astype(jnp.float32)
    obs_sum = jnp.dot(placed, received, precision=FULL)
    obs_count = jnp.sum(placed, axis=1)
    scale = 1.0 / (1.0 + obs_count[:, None] * gains[None, :])
    drive = gains[None, :] * obs_sum

    def block_compose(index, carry):
        total_map, total_shift = carry
        for inner in range(4):
            position = index * 4 + inner
            factor = lax.dynamic_index_in_dim(scale, position, 0, keepdims=False)
            forcing = lax.dynamic_index_in_dim(drive, position, 0, keepdims=False)
            total_map = factor[:, None] * jnp.dot(transition, total_map, precision=FULL)
            total_shift = factor * (jnp.dot(transition, total_shift, precision=FULL) + forcing)
        return (total_map, total_shift)

    identity = (jnp.eye(width, dtype=jnp.float32), jnp.zeros((width,), jnp.float32))
    own = lax.fori_loop(0, STEP_DEV // 4, block_compose, identity)
    seg_map, seg_shift = carried_in(own, "seg", compose, identity)
    inclusive = compose((seg_map, seg_shift), own)
    total_map, total_shift = (
        spread(inclusive[0], "seg", n_seg - 1),
        spread(inclusive[1], "seg", n_seg - 1),
    )
    grp_map, grp_shift = carried_in((total_map, total_shift), "grp", compose, identity)
    start = jnp.dot(grp_map, initial_state, precision=FULL) + grp_shift
    entry = jnp.dot(seg_map, start, precision=FULL) + seg_shift

    def block_states(index, carry):
        state, collected = carry
        for inner in range(4):
            position = index * 4 + inner
            factor = lax.dynamic_index_in_dim(scale, position, 0, keepdims=False)
            forcing = lax.dynamic_index_in_dim(drive, position, 0, keepdims=False)
            state = factor * (jnp.dot(transition, state, precision=FULL) + forcing)
            collected = lax.dynamic_update_index_in_dim(collected, state, position, 0)
        return (state, collected)

    empty = jnp.zeros((STEP_DEV, width), jnp.float32)
    final_state, collected = lax.fori_loop(0, STEP_DEV // 4, block_states, (entry, empty))
    return collected[None]


def solution(mesh):
    in_specs = (P(), P(), P(), P("grp", "seg", None), P("grp", "seg", None), P("grp", "seg"))
    out_specs = P("grp", "seg", None)
    return jax.shard_map(
        on_device, mesh=mesh, in_specs=in_specs, out_specs=out_specs, check_vma=False
    )
```

profile of v0, /device:TPU:31, one launch (start us, length us, event | category | flops | bytes accessed | tf_op | source)
XLA Modules:
  0.0 577.2 jit_solution(4149587804314496607)
XLA Ops:
  12.2 6.1 %all-to-all-start = ((f32[32,40,1]{1,2,0:T(1,128)}), f32[32,40,1]{1,2,0:T(1,128)S(1)}, u32[]{:S(2)}, u32[]{:S(2)}) async-start(f32[32,40,1]{1,2,0:T(1,128)} %bitcast.25), calls=%async_computation | async-start | bytes 32768 | tf_op jit(solution)/shard_map/all_to_all | solution.py:64
  18.3 3.9 scatter_custom_fusion.1
  22.3 6.7 %all-to-all-start.1 = ((f32[32,40,512]{2,1,0:T(8,128)}), f32[32,40,512]{2,1,0:T(8,128)}, u32[]{:S(2)}, u32[]{:S(2)}) async-start(f32[32,40,512]{2,1,0:T(8,128)} %bitcast.287), calls=%async_computation.1 | async-start | bytes 5242880 | tf_op jit(solution)/shard_map/all_to_all | solution.py:63
  31.9 55.7 %all-to-all-done.1 = f32[32,40,512]{2,1,0:T(8,128)} async-done(((f32[32,40,512]{2,1,0:T(8,128)}), f32[32,40,512]{2,1,0:T(8,128)}, u32[]{:S(2)}, u32[]{:S(2)}) %all-to-all-start.1) | async-done | bytes 2621472 | tf_op jit(solution)/shard_map/all_to_all | solution.py:63
  90.4 122.5 %while.68 = (s32[]{:T(128)}, f32[512,512]{0,1:T(8,128)}, f32[512]{0:T(512)S(1)}, f32[32,512]{1,0:T(8,128)S(1)}, f32[512,512]{1,0:T(8,128)S(1)}, /*index=5*/f32[3...) while((s32[]{:T(128)}, f32[512,512]{0,1:T(8,128)}, ...), condition=%wide.region_5.6_spmd.clone, body=%wide.region_4.5_spmd.clone.sunk | while | flops 6456087040 | bytes 16871776 | solution.py:84
  93.7 3.5 convolution_multiply_fusion.9
  109.0 3.5 convolution_multiply_fusion.9
  124.3 3.5 convolution_multiply_fusion.9
  136.4 3.1 convolution_multiply_fusion.8
  139.5 3.5 convolution_multiply_fusion.9
  154.8 3.5 convolution_multiply_fusion.9
  170.1 3.5 convolution_multiply_fusion.9
  185.3 3.5 convolution_multiply_fusion.9
  200.6 3.5 convolution_multiply_fusion.9
  214.0 21.4 %all-gather.2 = f32[8,1,512]{2,1,0:T(1,128)S(1)} all-gather(f32[1,1,512]{2,1,0:T(1,128)S(1)} %bitcast.335), channel_id=3, replica_groups=mesh['seg'=8,'grp'=4] {'seg'}, dimensions={0}, use_global_device_ids=true | all-gather | bytes 18432 | tf_op jit(solution)/shard_map/all_gather | solution.py:14
  235.4 100.8 %all-gather.9.cloned.1.call-done = f32[4096,512]{0,1:T(8,128)} async-done(((f32[512,512]{0,1:T(8,128)}), f32[4096,512]{0,1:T(8,128)}) %all-gather.9.cloned.1.call-update) | async-done | bytes 8388624 | tf_op jit(solution)/shard_map/all_gather | solution.py:14
  336.1 9.0 %copy.16 = f32[4096,512]{1,0:T(8,128)} copy(f32[4096,512]{0,1:T(8,128)} %all-gather.9.cloned.1.call-done) | data formatting | bytes 16777216 | tf_op jit(solution)/shard_map/all_gather | solution.py:14
  345.2 52.9 %while.69 = (s32[]{:T(128)}, f32[512,512]{1,0:T(8,128)}, f32[512]{0:T(512)S(1)}, s32[]{:T(128)}, f32[8,512,512]{2,1,0:T(8,128)}, /*index=5*/f32[8,512]{1,0:T(8,128)S(1)}, s32[]{:T(128)}, s32[]{:T(128)}) while((s32[]{:T(128)}, f32[512,512]{1,0:T(8,128)}, f32[512]{0:T(512)S(1)}, s32[]{:T(128)}, f32[8,512,512]{2,1,0:T(8,128)}, ...), condition=%wide.region_7.8_spmd.clone, body=%wide.region_6.7_spmd.clone.sunk | while | flops 1614022656 | bytes 7361647 | solution.py:23
  348.6 4.1 convolution_select_fusion.6
  356.2 4.1 convolution_select_fusion.6
  363.7 4.1 convolution_select_fusion.6
  371.3 4.1 convolution_select_fusion.6
  378.9 4.1 convolution_select_fusion.6
  386.4 4.1 convolution_select_fusion.6
  394.0 4.1 convolution_select_fusion.6
  398.1 4.4 fusion.15
  402.5 76.8 %all-reduce.2.cloned.1.call-done = f32[1,512,512]{2,1,0:T(8,128)} async-done(((f32[1,512,512]{2,1,0:T(8,128)}), f32[1,512,512]{2,1,0:T(8,128)}) %all-reduce.2.cloned.1.call-update) | async-done | bytes 1048592 | tf_op jit(solution)/shard_map/psum | solution.py:28
  481.2 13.4 %psum.15 = f32[1,512]{1,0:T(1,128)S(1)} all-reduce(f32[1,512]{1,0:T(1,128)S(1)} %bitcast.345), channel_id=1, replica_groups=mesh['seg'=8,'grp'=4] {'seg'}, use_global_device_ids=true, to_apply=%region_9.10 | all-reduce | flops 512 | bytes 4096 | tf_op jit(solution)/shard_map/psum | solution.py:28
  494.6 9.9 %all-gather.3 = f32[4,1,512]{2,1,0:T(1,128)S(1)} all-gather(f32[1,1,512]{2,1,0:T(1,128)S(1)} %bitcast.344), channel_id=1, replica_groups=mesh['seg'=8,'grp'=4] {'grp'}, dimensions={0}, use_global_device_ids=true | all-gather | bytes 10240 | tf_op jit(solution)/shard_map/all_gather | solution.py:14
  504.5 12.2 %all-gather.7.cloned.1.call-done = f32[4,512,512]{2,1,0:T(8,128)} async-done(((f32[1,512,512]{2,1,0:T(8,128)}), f32[4,512,512]{2,1,0:T(8,128)}) %all-gather.7.cloned.1.call-update) | async-done | bytes 4194320 | tf_op jit(solution)/shard_map/all_gather | solution.py:14
  516.7 16.3 %while.70 = (s32[]{:T(128)}, f32[512,512]{1,0:T(8,128)S(1)}, f32[512]{0:T(512)S(1)}, s32[]{:T(128)}, f32[4,512,512]{2,1,0:T(8,128)}, /*index=5*/f32[4,512]{1,0:T(4,128)S(1)}, s32[]{:T(128)}, s32[]{:T(128)}) while((s32[]{:T(128)}, f32[512,512]{1,0:T(8,128)S(1)}, f32[512]{0:T(512)S(1)}, s32[]{:T(128)}, f32[4,512,512]{2,1,0:T(8,128)}, ...), condition=%wide.region_11.12_spmd.clone, body=%wide.region_10.11_spmd.clone.sunk | while | flops 1614022656 | bytes 7361647 | solution.py:23
  536.2 33.8 %while.67 = (s32[]{:T(128)}, f32[512]{0:T(512)S(1)}, f32[32,512]{1,0:T(8,128)S(1)}, f32[32,512]{1,0:T(8,128)S(1)}, f32[512,512]{1,0:T(8,128)S(1)}, /*index=5*/f3...) while((s32[]{:T(128)}, f32[512]{0:T(512)S(1)}, ...), condition=%wide.region_13.14_spmd, body=%wide.region_12.13_spmd.sunk | while | flops 12587026 | bytes 4292965 | solution.py:106
  (305 shorter events, 182.6 us)
Async XLA Ops:
  6.5 11.8 %copy-start = (f32[1,512,512]{2,1,0:T(8,128)S(1)}, f32[1,512,512]{2,1,0:T(8,128)}, u32[]{:S(2)}) copy-start(f32[1,512,512]{2,1,0:T(8,128)} %param.17) | copy-start | bytes 3145732
  12.2 10.1 %all-to-all-start = ((f32[32,40,1]{1,2,0:T(1,128)}), f32[32,40,1]{1,2,0:T(1,128)S(1)}, u32[]{:S(2)}, u32[]{:S(2)}) async-start(f32[32,40,1]{1,2,0:T(1,128)} %bitcast.25), calls=%async_computation | async-start | bytes 32768 | tf_op jit(solution)/shard_map/all_to_all | solution.py:64
  22.3 9.6 %copy-start.3 = (f32[512]{0:T(512)S(1)}, f32[512]{0:T(512)}, u32[]{:S(2)}) copy-start(f32[512]{0:T(512)} %param.16) | copy-start | bytes 6148
  22.3 65.3 %all-to-all-start.1 = ((f32[32,40,512]{2,1,0:T(8,128)}), f32[32,40,512]{2,1,0:T(8,128)}, u32[]{:S(2)}, u32[]{:S(2)}) async-start(f32[32,40,512]{2,1,0:T(8,128)} %bitcast.287), calls=%async_computation.1 | async-start | bytes 5242880 | tf_op jit(solution)/shard_map/all_to_all | solution.py:63
  29.0 61.4 %copy-start.1 = (f32[512,512]{1,0:T(8,128)S(1)}, f32[512,512]{1,0:T(8,128)}, u32[]{:S(2)}) copy-start(f32[512,512]{1,0:T(8,128)} %param.15) | copy-start | bytes 3145732
  29.0 307.2 %all-gather.9.cloned.1.call-start = ((), (), s32[]{:S(2)}) async-start(), calls=%async_computation.4 | async-start | bytes 9437184 | tf_op jit(solution)/shard_map/all_gather | solution.py:14
  212.9 266.4 %all-reduce.2.cloned.1.call-start = ((), (), s32[]{:S(2)}) async-start(), calls=%async_computation.2 | async-start | bytes 2097152 | tf_op jit(solution)/shard_map/psum | solution.py:28
  402.4 114.2 %all-gather.7.cloned.1.call-start = ((), (), s32[]{:S(2)}) async-start(), calls=%async_computation.3 | async-start | bytes 5242880 | tf_op jit(solution)/shard_map/all_gather | solution.py:14
  516.7 16.3 %copy-start.4 = (f32[512]{0:T(512)S(1)}, f32[512]{0:T(512)}, u32[]{:S(2)}) copy-start(f32[512]{0:T(512)} %param.14) | copy-start | bytes 6148
  570.0 0.6 copy-start.2
Sparse Core Ops, SparseCore 0:
  213.0 123.0 all-gather.8
  402.6 76.6 all-reduce.1
  480.9 35.7 all-gather.6
where the time goes:
time: 581 us; the launch traced here: 577 us
  waiting for transfers between devices  245 us (42%)
  matrix products  224 us (39%)
  blocking collectives  44.7 us (8%)
  local copies, waits for them, and re-layouts  31 us (5%)
  between operations  13.3 us (2%)
  starting transfers between devices  13 us (2%)
    all_gather x2, waiting for transfers between devices, carried_in(): pieces = jax.tree.map(lambda part: lax.all_gather(part, axis), value)  113 us
    dot_general x32, matrix products, block_compose(): total_map = factor[:, None] * jnp.dot(transition, total_map, precision=FULL)  90.1 us
    psum x1, waiting for transfers between devices, spread(): return lax.psum(block, axis)  76.8 us
    all_to_all x1, waiting for transfers between devices, on_device(): lax.all_to_all(buffer, ('seg', 'grp'), split_axis=0, concat_axis=0, tiled...  55.7 us
    dot_general x11, matrix products, compose(): joined_map = jnp.dot(second_map, first_map, precision=FULL)  42.2 us
    all_gather x2, blocking collectives, carried_in(): pieces = jax.tree.map(lambda part: lax.all_gather(part, axis), value)  31.3 us
    dot_general x32, matrix products, block_compose(): jnp.dot(transition, total_shift, precision=FULL) + forcing  31.2 us
    dot_general x32, matrix products, block_states(): state = factor * (jnp.dot(transition, state, precision=FULL) + forcing)  30.9 us
  transfers between devices with their start and end apart: 5, of which 4 were waited for; matrix products, arithmetic and copies ran while one was open for 2% of the time, Pallas kernels for 0%

commit v1 on v0

v1 whole, which is shorter than its diff:
```python
import functools

import jax
import jax.numpy as jnp
from jax import lax
from jax.experimental import pallas as pl
from jax.experimental.pallas import tpu as pltpu
from jax.sharding import PartitionSpec as P

STEP_DEV = 32
PAIR = 2

F32 = jnp.float32
BF16 = jnp.bfloat16
HIGH = lax.Precision.HIGH
VMEM = pl.BlockSpec(memory_space=pltpu.VMEM)


def split(value):
    upper = value.astype(BF16)
    return upper, (value - upper.astype(F32)).astype(BF16)


def product(upper, lower, right_upper, right_lower):
    dot = functools.partial(jnp.dot, preferred_element_type=F32)
    return dot(upper, right_upper) + dot(lower, right_upper) + dot(upper, right_lower)


def row_times(row, matrix_ref):
    depth, width = matrix_ref.shape
    column = jnp.transpose(jnp.broadcast_to(row, (128, depth)))
    return jnp.concatenate(
        [
            jnp.sum(matrix_ref[:, at : at + 128] * column, axis=0, keepdims=True)
            for at in range(0, width, 128)
        ],
        axis=1,
    )


def map_kernel(moved_ref, scale_ref, half_ref, full_ref, upper_ref, lower_ref):
    share = full_ref.shape[0]
    side = lax.axis_index("seg") % PAIR
    upper, lower = split(moved_ref[...])
    upper_ref[...] = upper
    lower_ref[...] = lower
    rows = pl.ds(pl.multiple_of(side * share, share), share)
    full_ref[...] = moved_ref[rows, :] * scale_ref[pl.ds(0, 1), :]

    def step(at, carry):
        upper, lower = split(full_ref[...])
        joined = product(upper, lower, upper_ref[...], lower_ref[...])
        full_ref[...] = joined * scale_ref[pl.ds(at, 1), :]
        return carry

    lax.fori_loop(1, STEP_DEV, step, 0)
    half_ref[...] = full_ref[...]
    lax.fori_loop(STEP_DEV, PAIR * STEP_DEV, step, 0)


def pair_maps(moved, scale):
    width = moved.shape[0]
    share = width // PAIR
    shape = jax.ShapeDtypeStruct((share, width), F32)
    return pl.pallas_call(
        map_kernel,
        out_shape=(shape, shape),
        in_specs=[VMEM, VMEM],
        out_specs=(VMEM, VMEM),
        scratch_shapes=[pltpu.VMEM((width, width), BF16), pltpu.VMEM((width, width), BF16)],
        compiler_params=pltpu.CompilerParams(vmem_limit_bytes=24 << 20),
        cost_estimate=pl.CostEstimate(
            flops=PAIR * STEP_DEV * 6 * share * width * width,
            bytes_accessed=8 * width * width,
            transcendentals=0,
        ),
    )(moved, scale)


def chain_kernel(
    n_seg,
    n_dev,
    initial_ref,
    moved_ref,
    scale_ref,
    drive_ref,
    half_ref,
    full_ref,
    out_ref,
    into_ref,
    mid_in_ref,
    send_ref,
    mid_send_ref,
    shift_ref,
    state_ref,
    into_sem,
    mid_sem,
    send_sem,
    mid_send_sem,
):
    me = lax.axis_index("grp") * n_seg + lax.axis_index("seg")
    side = me % PAIR
    pair = me // PAIR
    n_pair = n_dev // PAIR
    share = half_ref.shape[0]

    def place(index):
        return {"grp": index // n_seg, "seg": index % n_seg}

    mate = pair * PAIR + 1 - side
    barrier = pltpu.get_barrier_semaphore()
    pl.semaphore_signal(barrier, inc=1, device_id=place(mate))
    for other in range(PAIR):

        @pl.when(pair > 0)
        def _():
            pl.semaphore_signal(barrier, inc=1, device_id=place((pair - 1) * PAIR + other))

        @pl.when(pair < n_pair - 1)
        def _():
            pl.semaphore_signal(barrier, inc=1, device_id=place((pair + 1) * PAIR + other))

    behind = (pair + n_pair - 1) // n_pair
    ahead = 1 - (pair + 1) // n_pair
    pl.semaphore_wait(barrier, 1 + PAIR * (behind + ahead))

    def forced(at, row):
        moved = row_times(row, moved_ref) + drive_ref[pl.ds(at, 1), :]
        return moved * scale_ref[pl.ds(side * STEP_DEV + at, 1), :]

    def unforced(at, row):
        return row_times(row, moved_ref) * scale_ref[pl.ds(at, 1), :]

    shift = lax.fori_loop(0, STEP_DEV, forced, jnp.zeros_like(initial_ref))
    shift_ref[0:1, :] = shift
    shift = lax.fori_loop(STEP_DEV, STEP_DEV + (1 - side) * STEP_DEV, unforced, shift)
    shift_ref[1:2, :] = shift

    @pl.when(pair == 0)
    def _():
        state_ref[...] = initial_ref[...]

    def chain_copy(source, other):
        return pltpu.make_async_remote_copy(
            src_ref=send_ref,
            dst_ref=into_ref.at[source],
            send_sem=send_sem.at[other],
            recv_sem=into_sem.at[source],
            device_id=place((pair + 1) * PAIR + other),
        )

    def mid_copy():
        return pltpu.make_async_remote_copy(
            src_ref=mid_send_ref,
            dst_ref=mid_in_ref,
            send_sem=mid_send_sem,
            recv_sem=mid_sem,
            device_id=place(mate),
        )

    @pl.when(pair > 0)
    def _():
        for source in range(PAIR):
            pltpu.make_async_copy(into_ref.at[source], into_ref.at[source], into_sem.at[source]).wait()
        state_ref[...] = into_ref[0] + into_ref[1]

    mine = state_ref[:, pl.ds(pl.multiple_of(side * share, share), share)]

    @pl.when(pair < n_pair - 1)
    def _():
        send_ref[...] = row_times(mine, full_ref) + shift_ref[1:2, :]
        for source in range(PAIR):

            @pl.when(side == source)
            def _():
                for other in range(PAIR):
                    chain_copy(source, other).start()

    middle = row_times(mine, half_ref)

    @pl.when(side == 0)
    def _():
        mid_send_ref[...] = middle + shift_ref[0:1, :]
        mid_copy().start()
        mid_copy().wait_send()

    @pl.when(side == 1)
    def _():
        pltpu.make_async_copy(mid_in_ref, mid_in_ref, mid_sem).wait()
        state_ref[...] = middle + mid_in_ref[...]

    def advance(at, row):
        row = forced(at, row)
        out_ref[pl.ds(at, 1), :] = row
        return row

    lax.fori_loop(0, STEP_DEV, advance, state_ref[...])

    @pl.when(pair < n_pair - 1)
    def _():
        for other in range(PAIR):
            pltpu.make_async_copy(send_ref, send_ref, send_sem.at[other]).wait()


def chain(n_seg, n_dev, initial, moved, scale, drive, half, full):
    width = moved.shape[0]
    row = pltpu.VMEM((1, width), F32)
    return pl.pallas_call(
        functools.partial(chain_kernel, n_seg, n_dev),
        out_shape=jax.ShapeDtypeStruct((STEP_DEV, width), F32),
        in_specs=[VMEM] * 6,
        out_specs=VMEM,
        scratch_shapes=[
            pltpu.VMEM((PAIR, 1, width), F32),
            row,
            row,
            row,
            pltpu.VMEM((2, width), F32),
            row,
            pltpu.SemaphoreType.DMA((PAIR,)),
            pltpu.SemaphoreType.DMA,
            pltpu.SemaphoreType.DMA((PAIR,)),
            pltpu.SemaphoreType.DMA,
        ],
        compiler_params=pltpu.CompilerParams(
            collective_id=0, has_side_effects=True, vmem_limit_bytes=24 << 20
        ),
    )(initial, moved, scale, drive, half, full)


def on_device(initial_state, transition, gains, tiles, tile_owner, tile_step):
    n_seg = lax.axis_size("seg")
    n_grp = lax.axis_size("grp")
    n_dev = n_seg * n_grp
    me = lax.axis_index("grp") * n_seg + lax.axis_index("seg")
    where_step = tile_owner[0, :, 0] * STEP_DEV + tile_step[0]
    bins = jnp.arange(n_dev * STEP_DEV, dtype=jnp.int32)
    placed = (bins[:, None] == where_step[None, :]).astype(F32)
    counts = lax.psum(jnp.sum(placed, axis=1).reshape(-1, 128), ("grp", "seg")).reshape(-1)
    sums = lax.psum_scatter(
        jnp.dot(placed, tiles[0], precision=HIGH), ("grp", "seg"), scatter_dimension=0, tiled=True
    )
    span = PAIR * STEP_DEV
    pair_counts = lax.dynamic_slice_in_dim(counts, me // PAIR * span, span)
    scale = 1.0 / (1.0 + pair_counts[:, None] * gains[None, :])
    moved = transition.T
    half, full = pair_maps(moved, scale)
    drive = gains[None, :] * sums
    states = chain(n_seg, n_dev, initial_state[None], moved, scale, drive, half, full)
    return states[None]


def solution(mesh):
    in_specs = (P(), P(), P(), P("grp", "seg", None), P("grp", "seg", None), P("grp", "seg"))
    out_specs = P("grp", "seg", None)
    return jax.shard_map(
        on_device, mesh=mesh, in_specs=in_specs, out_specs=out_specs, check_vma=False
    )
```

time: 581 us -> 217 us (0.37)
  matrix products: 224 us -> 2.64 us
  waiting for transfers between devices: 245 us -> 58.5 us
  Pallas kernels: 0 us -> 100 us
  local copies, waits for them, and re-layouts: 31 us -> 1.51 us
  starting transfers between devices: 13 us -> 0.01 us
  blocking collectives: 44.7 us -> 38.6 us
    dot_general x122 -> x1, matrix products: 224 us -> 2.64 us  [on_device(): jnp.dot(placed, tiles[0], precision=HIGH)]
    all_gather x2 -> x0, waiting for transfers between devices: 113 us -> none  [carried_in(): pieces = jax.tree.map(lambda part: lax.all_gather(part, axis), value)]
    pallas_call x0 -> x2, Pallas kernels: none -> 100 us  [the longest x1 63.2 us: chain(): pl.pallas_call(functools.partial(chain_kernel, n_seg, n_dev), out_shape=j...]
    psum x1 -> x0, waiting for transfers between devices: 76.8 us -> none  [spread(): return lax.psum(block, axis)]
    reduce_scatter x0 -> x1, waiting for transfers between devices: none -> 58.5 us  [on_device(): lax.psum_scatter(jnp.dot(placed, tiles[0], precision=HIGH), ('grp', 'seg'...]
    all_to_all x2 -> x0, waiting for transfers between devices: 55.7 us -> none  [the longest x1 55.7 us: on_device(): lax.all_to_all(buffer, ('seg', 'grp'), split_axis=0, concat_axis=0, tiled...]
    all_gather x2 -> x0, blocking collectives: 31.3 us -> none  [carried_in(): pieces = jax.tree.map(lambda part: lax.all_gather(part, axis), value)]
    psum x1, blocking collectives: 13.4 us -> 38.6 us  [on_device(): lax.psum(jnp.sum(placed, axis=1).reshape(-1, 128), ('grp', 'seg'))]
  transfers between devices with their start and end apart: 5 -> 1, of which waited for: 4 -> 1; matrix products, arithmetic and copies ran while one was open for 2% -> 0% of each run, Pallas kernels for 0% -> 17%
where the time goes in v1:
time: 217 us
  Pallas kernels  100 us (46%)
  waiting for transfers between devices  58.5 us (27%)
  blocking collectives  38.6 us (18%)
  between operations  13.5 us (6%)
  matrix products  2.64 us (1%)
    pallas_call x1, Pallas kernels, chain(): pl.pallas_call(functools.partial(chain_kernel, n_seg, n_dev), out_shape=j...  63.2 us
    reduce_scatter x1, waiting for transfers between devices, on_device(): lax.psum_scatter(jnp.dot(placed, tiles[0], precision=HIGH), ('grp', 'seg'...  58.5 us
    psum x1, blocking collectives, on_device(): lax.psum(jnp.sum(placed, axis=1).reshape(-1, 128), ('grp', 'seg'))  38.6 us
    pallas_call x1, Pallas kernels, pair_maps(): pl.pallas_call(map_kernel, out_shape=(shape, shape), in_specs=[VMEM, VMEM...  37.2 us
  transfers between devices with their start and end apart: 1, of which 1 were waited for; matrix products, arithmetic and copies ran while one was open for 0% of the time, Pallas kernels for 17%

profile of v1, /device:TPU:31, one launch (start us, length us, event | category | flops | bytes accessed | tf_op | source)
XLA Modules:
  0.0 217.1 jit_solution(1494798100565140350)
XLA Ops:
  6.5 0.0 copy-start
  6.5 0.0 reduce-scatter.2.cloned.1.call-start
  6.5 0.8 bitcast_add_fusion
  7.3 0.5 copy-done
  7.8 0.0 copy-start.2
  7.8 2.6 %fusion = f32[1024,512]{1,0:T(8,128)} fusion(f32[1,512,512]{2,1,0:T(8,128)S(1)} %copy-done, s32[512]{0:T(512)S(1)} %bitcast.13), kind=kOutput, calls=%fused_computation.2 | convolution fusion | flops 1611137024 | bytes 3147776 | tf_op jit(solution)/shard_map/dot_general | solution.py:241
  10.4 0.0 copy-start.3
  10.4 0.0 reduce-scatter.2.cloned.1.call-update
  10.5 0.0 copy-done.2
  10.5 0.3 copy.8
  10.8 0.3 convert_reduce_fusion
  11.1 38.6 %psum.7 = f32[1024]{0:T(1024)S(1)} all-reduce(f32[1024]{0:T(1024)S(1)} %convert_reduce_fusion), channel_id=1, replica_groups=mesh['seg'=8,'grp'=4] {'grp','seg'}, use_global_device_ids=true, to_apply=%region_1.0 | all-reduce | flops 1024 | bytes 8192 | tf_op jit(solution)/shard_map/psum | solution.py:239
  49.7 0.1 dynamic_slice.3
  49.8 0.0 copy-done.3
  49.8 0.1 add_divide_fusion.scale_ref
  49.9 0.0 copy-start.1
  49.9 37.2 %shard_map.64 = (f32[256,512]{1,0:T(8,128)S(1)}, f32[256,512]{1,0:T(8,128)S(1)}) custom-call(f32[512,512]{1,0:T(8,128)S(1)} %bitcast.9, f32[64,512]{1,0:T(8,128)S(1)} %add_divide_fusion.scale_ref), custom_call_target="tpu_custom_call" | custom-call | flops 25769803776 | bytes 2097152 | tf_op jit(solution)/shard_map/pallas_call | solution.py:65
  87.0 58.5 %reduce-scatter.2.cloned.1.call-done = f32[32,512]{1,0:T(8,128)} async-done(((f32[1024,512]{1,0:T(8,128)}), f32[32,512]{1,0:T(8,128)}) %reduce-scatter.2.cloned.1.call-update) | async-done | bytes 65552 | tf_op jit(solution)/shard_map/reduce_scatter | solution.py:240
  145.5 0.8 broadcast_multiply_fusion.drive_ref
  146.4 0.0 copy-done.1
  146.4 63.2 %shard_map.65 = f32[32,512]{1,0:T(8,128)S(1)} custom-call(f32[1,512]{1,0:T(1,128)S(1)} %bitcast.12, f32[512,512]{1,0:T(8,128)S(1)} %bitcast.10, f32[64,512]{1,0:T(8,128)S(1)} %add_divide_fusion.scale_ref, f32[32,512]{1,0:T(8,128)S(1)} %broadcast_multiply_fusion.drive_ref, f32[256,512]{1,0:T(8,128)S(1)} %get-tuple-element.7.half_ref, ...), custom_call_target="tpu_custom_call" | custom-call | tf_op jit(solution)/shard_map/pallas_call | solution.py:208
  209.6 0.6 copy.10
Async XLA Ops:
  6.5 1.3 copy-start
  6.5 139.0 %reduce-scatter.2.cloned.1.call-start = ((), (), s32[]{:S(2)}) async-start(), calls=%async_computation.1 | async-start | bytes 2162688 | tf_op jit(solution)/shard_map/reduce_scatter | solution.py:240
  7.8 2.7 %copy-start.2 = (f32[512,512]{1,0:T(8,128)S(1)}, f32[512,512]{1,0:T(8,128)}, u32[]{:S(2)}) copy-start(f32[512,512]{1,0:T(8,128)} %param.7) | copy-start | bytes 3145732
  10.4 39.3 %copy-start.3 = (f32[512]{0:T(512)S(1)}, f32[512]{0:T(512)}, u32[]{:S(2)}) copy-start(f32[512]{0:T(512)} %param.8) | copy-start | bytes 6148
  49.9 96.5 %copy-start.1 = (f32[512]{0:T(512)S(1)}, f32[512]{0:T(512)}, u32[]{:S(2)}) copy-start(f32[512]{0:T(512)} %param.6) | copy-start | bytes 6148
Sparse Core Ops, SparseCore 0:
  10.6 134.8 reduce-scatter.1

commit v2 on v1

v2 whole, which is shorter than its diff:
```python
import functools

import jax
import jax.numpy as jnp
from jax import lax
from jax.experimental import pallas as pl
from jax.experimental.pallas import tpu as pltpu
from jax.sharding import PartitionSpec as P

STEP_DEV = 32
PAIR = 2

F32 = jnp.float32
BF16 = jnp.bfloat16
VMEM = pl.BlockSpec(memory_space=pltpu.VMEM)


def split(value):
    upper = value.astype(BF16)
    return upper, (value - upper.astype(F32)).astype(BF16)


def product(upper, lower, right_upper, right_lower):
    dot = functools.partial(jnp.dot, preferred_element_type=F32)
    return dot(upper, right_upper) + dot(lower, right_upper) + dot(upper, right_lower)


def row_times(row, matrix_ref):
    depth, width = matrix_ref.shape
    column = jnp.transpose(jnp.broadcast_to(row, (128, depth)))
    return jnp.concatenate(
        [
            jnp.sum(matrix_ref[:, at : at + 128] * column, axis=0, keepdims=True)
            for at in range(0, width, 128)
        ],
        axis=1,
    )


def filter_kernel(
    n_seg,
    n_grp,
    initial_ref,
    moved_ref,
    gains_ref,
    counts_ref,
    where_ref,
    tiles_ref,
    out_ref,
    upper_ref,
    lower_ref,
    full_ref,
    half_ref,
    scale_ref,
    drive_ref,
    tile_upper_ref,
    tile_lower_ref,
    counts_in_ref,
    plane_out_ref,
    plane_in_ref,
    plane_sum_ref,
    line_in_ref,
    into_ref,
    mid_in_ref,
    send_ref,
    mid_send_ref,
    shift_ref,
    state_ref,
    counts_sems,
    plane_sems,
    line_sems,
    into_sem,
    mid_sem,
    send_sem,
    mid_send_sem,
):
    n_dev = n_seg * n_grp
    depth = line_in_ref.shape[0] + 1
    inner = n_seg // depth
    n_plane = inner * n_grp
    seg, grp = lax.axis_index("seg"), lax.axis_index("grp")
    me = grp * n_seg + seg
    side = me % PAIR
    pair = me // PAIR
    mate = pair * PAIR + 1 - side
    n_pair = n_dev // PAIR
    share, width = full_ref.shape
    level, spot = seg // inner, grp * inner + seg % inner

    def place(index):
        return {"grp": index // n_seg, "seg": index % n_seg}

    barrier = pltpu.get_barrier_semaphore()

    def greet(at, carry):
        pl.semaphore_signal(barrier, inc=1, device_id=place((me + 1 + at) % n_dev))
        return carry

    lax.fori_loop(0, n_dev - 1, greet, 0)

    row_ids = lax.broadcasted_iota(jnp.int32, (width, width), 0)
    column_ids = lax.broadcasted_iota(jnp.int32, (width, width), 1)
    on_diagonal = row_ids == column_ids
    diagonal = jnp.sum(jnp.where(on_diagonal, moved_ref[...], 0.0), axis=0, keepdims=True)
    upper, lower = split(jnp.where(on_diagonal, 0.0, moved_ref[...]))
    upper_ref[...] = upper
    lower_ref[...] = lower
    upper, lower = split(tiles_ref[...])
    tile_upper_ref[...] = upper
    tile_lower_ref[...] = lower
    pl.semaphore_wait(barrier, n_dev - 1)

    def send_counts(at, carry):
        other = (me + 1 + at) % n_dev
        pltpu.make_async_remote_copy(
            src_ref=counts_ref.at[other // PAIR],
            dst_ref=counts_in_ref.at[at],
            send_sem=counts_sems.at[0],
            recv_sem=counts_sems.at[1],
            device_id=place(other),
        ).start()
        return carry

    lax.fori_loop(0, n_dev - 1, send_counts, 0)

    def binned(other):
        rows = lax.broadcasted_iota(jnp.int32, (depth * STEP_DEV, 1), 0)
        owner = (other // inner) * n_seg + (rows // STEP_DEV) * inner + other % inner
        placed = (owner * STEP_DEV + rows % STEP_DEV == where_ref[...]).astype(F32).astype(BF16)
        dot = functools.partial(jnp.dot, preferred_element_type=F32)
        return dot(placed, tile_upper_ref[...]) + dot(placed, tile_lower_ref[...])

    def send_plane(at, carry):
        other = (spot + 1 + at) % n_plane
        plane_out_ref[at] = binned(other)
        pltpu.make_async_remote_copy(
            src_ref=plane_out_ref.at[at],
            dst_ref=plane_in_ref.at[at],
            send_sem=plane_sems.at[0],
            recv_sem=plane_sems.at[1],
            device_id={"grp": other // inner, "seg": level * inner + other % inner},
        ).start()
        return carry

    lax.fori_loop(0, n_plane - 1, send_plane, 0)
    plane_sum_ref[...] = binned(spot)

    def landed(ref, sem):
        pltpu.make_async_copy(ref, ref, sem).wait()

    landed(counts_in_ref, counts_sems.at[1])
    counts = counts_ref[pair] + jnp.sum(counts_in_ref[...], axis=0)
    column = jnp.transpose(jnp.broadcast_to(counts, (128, 128)))[: PAIR * STEP_DEV]
    for at in range(0, width, 128):
        scale_ref[:, at : at + 128] = 1.0 / (1.0 + column * gains_ref[:, at : at + 128])

    rows = pl.ds(pl.multiple_of(side * share, share), share)
    full_ref[...] = moved_ref[rows, :] * scale_ref[pl.ds(0, 1), :]

    def step(at, carry):
        upper, lower = split(full_ref[...])
        joined = product(upper, lower, upper_ref[...], lower_ref[...])
        full_ref[...] = (joined + full_ref[...] * diagonal) * scale_ref[pl.ds(at, 1), :]
        return carry

    lax.fori_loop(1, STEP_DEV, step, 0)
    half_ref[...] = full_ref[...]
    lax.fori_loop(STEP_DEV, STEP_DEV + STEP_DEV // 4, step, 0)

    landed(plane_in_ref, plane_sems.at[1])
    plane_sum_ref[...] += jnp.sum(plane_in_ref[...], axis=0)

    def level_rows(index):
        return pl.ds(pl.multiple_of(index * STEP_DEV, STEP_DEV), STEP_DEV)

    def send_line(at, carry):
        other = (level + 1 + at) % depth
        pltpu.make_async_remote_copy(
            src_ref=plane_sum_ref.at[level_rows(other)],
            dst_ref=line_in_ref.at[at],
            send_sem=line_sems.at[0],
            recv_sem=line_sems.at[1],
            device_id={"grp": grp, "seg": other * inner + seg % inner},
        ).start()
        return carry

    lax.fori_loop(0, depth - 1, send_line, 0)
    lax.fori_loop(STEP_DEV + STEP_DEV // 4, PAIR * STEP_DEV, step, 0)
    landed(line_in_ref, line_sems.at[1])
    sums = plane_sum_ref[level_rows(level), :] + jnp.sum(line_in_ref[...], axis=0)
    drive_ref[...] = gains_ref[...] * sums

    def forced(at, row):
        moved = row_times(row, moved_ref) + drive_ref[pl.ds(at, 1), :]
        return moved * scale_ref[pl.ds(side * STEP_DEV + at, 1), :]

    def unforced(at, row):
        return row_times(row, moved_ref) * scale_ref[pl.ds(at, 1), :]

    shift = lax.fori_loop(0, STEP_DEV, forced, jnp.zeros_like(initial_ref))
    shift_ref[0:1, :] = shift
    shift = lax.fori_loop(STEP_DEV, STEP_DEV + (1 - side) * STEP_DEV, unforced, shift)
    shift_ref[1:2, :] = shift

    @pl.when(pair == 0)
    def _():
        state_ref[...] = initial_ref[...]

    def chain_copy(source, other):
        return pltpu.make_async_remote_copy(
            src_ref=send_ref,
            dst_ref=into_ref.at[source],
            send_sem=send_sem.at[other],
            recv_sem=into_sem.at[source],
            device_id=place((pair + 1) * PAIR + other),
        )

    def mid_copy():
        return pltpu.make_async_remote_copy(
            src_ref=mid_send_ref,
            dst_ref=mid_in_ref,
            send_sem=mid_send_sem,
            recv_sem=mid_sem,
            device_id=place(mate),
        )

    @pl.when(pair > 0)
    def _():
        for source in range(PAIR):
            pltpu.make_async_copy(into_ref.at[source], into_ref.at[source], into_sem.at[source]).wait()
        state_ref[...] = into_ref[0] + into_ref[1]

    mine = state_ref[:, pl.ds(pl.multiple_of(side * share, share), share)]

    @pl.when(pair < n_pair - 1)
    def _():
        send_ref[...] = row_times(mine, full_ref) + shift_ref[1:2, :]
        for source in range(PAIR):

            @pl.when(side == source)
            def _():
                for other in range(PAIR):
                    chain_copy(source, other).start()

    middle = row_times(mine, half_ref)

    @pl.when(side == 0)
    def _():
        mid_send_ref[...] = middle + shift_ref[0:1, :]
        mid_copy().start()
        mid_copy().wait_send()

    @pl.when(side == 1)
    def _():
        pltpu.make_async_copy(mid_in_ref, mid_in_ref, mid_sem).wait()
        state_ref[...] = middle + mid_in_ref[...]

    def advance(at, row):
        row = forced(at, row)
        out_ref[pl.ds(at, 1), :] = row
        return row

    lax.fori_loop(0, STEP_DEV, advance, state_ref[...])

    @pl.when(pair < n_pair - 1)
    def _():
        for other in range(PAIR):
            pltpu.make_async_copy(send_ref, send_ref, send_sem.at[other]).wait()
    landed(counts_in_ref, counts_sems.at[0])
    landed(plane_out_ref, plane_sems.at[0])
    landed(line_in_ref, line_sems.at[0])


def filtered(n_seg, n_grp, initial, moved, gains, counts, where_step, tiles):
    n_dev = n_seg * n_grp
    depth = 4
    n_plane = n_dev // depth
    tile_count, width = tiles.shape
    share = width // PAIR
    row = pltpu.VMEM((1, width), F32)
    return pl.pallas_call(
        functools.partial(filter_kernel, n_seg, n_grp),
        out_shape=jax.ShapeDtypeStruct((STEP_DEV, width), F32),
        in_specs=[VMEM] * 6,
        out_specs=VMEM,
        scratch_shapes=[
            pltpu.VMEM((width, width), BF16),
            pltpu.VMEM((width, width), BF16),
            pltpu.VMEM((share, width), F32),
            pltpu.VMEM((share, width), F32),
            pltpu.VMEM((PAIR * STEP_DEV, width), F32),
            pltpu.VMEM((STEP_DEV, width), F32),
            pltpu.VMEM((tile_count, width), BF16),
            pltpu.VMEM((tile_count, width), BF16),
            pltpu.VMEM((n_dev - 1, 1, 128), F32),
            pltpu.VMEM((n_plane - 1, depth * STEP_DEV, width), F32),
            pltpu.VMEM((n_plane - 1, depth * STEP_DEV, width), F32),
            pltpu.VMEM((depth * STEP_DEV, width), F32),
            pltpu.VMEM((depth - 1, STEP_DEV, width), F32),
            pltpu.VMEM((PAIR, 1, width), F32),
            row,
            row,
            row,
            pltpu.VMEM((2, width), F32),
            row,
            pltpu.SemaphoreType.DMA((2,)),
            pltpu.SemaphoreType.DMA((2,)),
            pltpu.SemaphoreType.DMA((2,)),
            pltpu.SemaphoreType.DMA((PAIR,)),
            pltpu.SemaphoreType.DMA,
            pltpu.SemaphoreType.DMA((PAIR,)),
            pltpu.SemaphoreType.DMA,
        ],
        compiler_params=pltpu.CompilerParams(
            collective_id=0, has_side_effects=True, vmem_limit_bytes=48 << 20
        ),
    )(initial, moved, gains, counts, where_step, tiles)


def on_device(initial_state, transition, gains, tiles, tile_owner, tile_step):
    n_seg = lax.axis_size("seg")
    n_grp = lax.axis_size("grp")
    where_step = tile_owner[0, :, 0] * STEP_DEV + tile_step[0]
    bins = jnp.arange(n_seg * n_grp * STEP_DEV, dtype=jnp.int32)
    counts = jnp.sum((bins[:, None] == where_step[None, :]).astype(F32), axis=1)
    counts = counts.reshape(-1, 1, PAIR * STEP_DEV)
    counts = jnp.pad(counts, ((0, 0), (0, 0), (0, 128 - PAIR * STEP_DEV)))
    states = filtered(
        n_seg,
        n_grp,
        initial_state[None],
        transition.T,
        gains[None],
        counts,
        where_step[None],
        tiles[0],
    )
    return states[None]


def solution(mesh):
    in_specs = (P(), P(), P(), P("grp", "seg", None), P("grp", "seg", None), P("grp", "seg"))
    out_specs = P("grp", "seg", None)
    return jax.shard_map(
        on_device, mesh=mesh, in_specs=in_specs, out_specs=out_specs, check_vma=False
    )
```

time: 217 us -> 108 us (0.50)
  waiting for transfers between devices: 58.5 us -> 0 us
  blocking collectives: 38.6 us -> 0 us
  between operations: 13.5 us -> 0.07 us
  Pallas kernels: 100 us -> 105 us
  matrix products: 2.64 us -> 0 us
    reduce_scatter x1 -> x0, waiting for transfers between devices: 58.5 us -> none  [on_device(): lax.psum_scatter(jnp.dot(placed, tiles[0], precision=HIGH), ('grp', 'seg'...]
    psum x1 -> x0, blocking collectives: 38.6 us -> none  [on_device(): lax.psum(jnp.sum(placed, axis=1).reshape(-1, 128), ('grp', 'seg'))]
    pallas_call x2 -> x1, Pallas kernels: 100 us -> 105 us  [filtered(): pl.pallas_call(functools.partial(filter_kernel, n_seg, n_grp), out_shape=...]
    dot_general x1 -> x0, matrix products: 2.64 us -> none  [on_device(): jnp.dot(placed, tiles[0], precision=HIGH)]
  transfers between devices with their start and end apart: 1 -> 0, of which waited for: 1 -> 0; matrix products, arithmetic and copies ran while one was open for 0% -> 0% of each run, Pallas kernels for 17% -> 0%
where the time goes in v2:
time: 108 us
  Pallas kernels  105 us (97%)
  local copies, waits for them, and re-layouts  2.38 us (2%)
    pallas_call x1, Pallas kernels, filtered(): pl.pallas_call(functools.partial(filter_kernel, n_seg, n_grp), out_shape=...  105 us
    unnamed x8, local copies, waits for them, and re-layouts  2.29 us

profile of v2, /device:TPU:31, one launch (start us, length us, event | category | flops | bytes accessed | tf_op | source)
XLA Modules:
  0.0 108.1 jit_solution(10198565831640284448)
XLA Ops:
  0.0 0.7 bitcast_add_fusion.where_ref
  0.7 0.3 convert_reduce_fusion
  1.0 0.1 reshape.15
  1.1 0.0 copy-start
  1.1 0.0 copy-start.1
  1.1 0.0 copy-start.2
  1.1 1.6 %copy.8 = f32[512,512]{0,1:T(8,128)S(1)} copy(f32[512,512]{1,0:T(8,128)} %param.7) | data formatting | bytes 2097152 | tf_op args[1]
  2.8 0.0 copy-done
  2.8 0.0 copy-done.1
  2.8 0.0 copy-done.2
  2.8 104.7 %shard_map.64 = f32[32,512]{1,0:T(8,128)S(1)} custom-call(f32[1,512]{1,0:T(1,128)S(1)} %bitcast.12, f32[512,512]{1,0:T(8,128)S(1)} %bitcast.8, f32[1,512]{1,0:T(1,128)S(1)} %bitcast.13, f32[16,1,128]{2,1,0:T(1,128)S(1)} %pad.4.counts_ref, s32[1,512]{1,0:T(1,128)S(1)} %bitcast_add_fusion.where_ref, f32[512,512]{1,0:T(8,128)S(1)} %bitcast.9), custom_call_target="tpu_custom_call" | custom-call | tf_op jit(solution)/shard_map/pallas_call | solution.py:281
  107.5 0.6 copy.10
  (1 shorter events, 0.0 us)
Async XLA Ops:
  1.1 1.7 %copy-start = (f32[1,512,512]{2,1,0:T(8,128)S(1)}, f32[1,512,512]{2,1,0:T(8,128)}, u32[]{:S(2)}) copy-start(f32[1,512,512]{2,1,0:T(8,128)} %param.9) | copy-start | bytes 3145732
  1.1 1.7 %copy-start.1 = (f32[512]{0:T(512)S(1)}, f32[512]{0:T(512)}, u32[]{:S(2)}) copy-start(f32[512]{0:T(512)} %param.6) | copy-start | bytes 6148
  1.1 1.7 %copy-start.2 = (f32[512]{0:T(512)S(1)}, f32[512]{0:T(512)}, u32[]{:S(2)}) copy-start(f32[512]{0:T(512)} %param.8) | copy-start | bytes 6148

commit v3 on v2

--- a/solution.py
+++ b/solution.py
@@ -9,6 +9,7 @@
 
 STEP_DEV = 32
 PAIR = 2
+FIRST = 4
 
 F32 = jnp.float32
 BF16 = jnp.bfloat16
@@ -41,6 +42,7 @@
     n_seg,
     n_grp,
     initial_ref,
+    transition_ref,
     moved_ref,
     gains_ref,
     counts_ref,
@@ -52,7 +54,12 @@
     full_ref,
     half_ref,
     scale_ref,
+    column_ref,
+    gains_column_ref,
+    factors_ref,
     drive_ref,
+    drive_columns_ref,
+    between_ref,
     tile_upper_ref,
     tile_lower_ref,
     counts_in_ref,
@@ -108,6 +115,7 @@
     upper, lower = split(tiles_ref[...])
     tile_upper_ref[...] = upper
     tile_lower_ref[...] = lower
+    gains_column_ref[...] = jnp.transpose(jnp.broadcast_to(gains_ref[...], (128, width)))
     pl.semaphore_wait(barrier, n_dev - 1)
 
     def send_counts(at, carry):
@@ -154,18 +162,36 @@
     for at in range(0, width, 128):
         scale_ref[:, at : at + 128] = 1.0 / (1.0 + column * gains_ref[:, at : at + 128])
 
+    half_share = share // 2
     rows = pl.ds(pl.multiple_of(side * share, share), share)
     full_ref[...] = moved_ref[rows, :] * scale_ref[pl.ds(0, 1), :]
-
-    def step(at, carry):
-        upper, lower = split(full_ref[...])
-        joined = product(upper, lower, upper_ref[...], lower_ref[...])
-        full_ref[...] = (joined + full_ref[...] * diagonal) * scale_ref[pl.ds(at, 1), :]
-        return carry
-
-    lax.fori_loop(1, STEP_DEV, step, 0)
+    column_ref[...] = column
+
+    def tabulate(entry):
+        count = column_ref[pl.ds(2 * entry, 1), :]
+        factors_ref[entry] = 1.0 / (1.0 + count * gains_column_ref[...])
+
+    def advance_maps(first, count, entries):
+        parts = [full_ref[at : at + half_share, :] for at in (0, half_share)]
+        for ahead in range(count):
+            factor = scale_ref[pl.ds(first + ahead, 1), :]
+            for at in range(2):
+                upper, lower = split(parts[at])
+                joined = product(upper, lower, upper_ref[...], lower_ref[...])
+                parts[at] = (joined + parts[at] * diagonal) * factor
+            if ahead < entries:
+                tabulate(first + ahead - FIRST)
+        for at in range(2):
+            full_ref[at * half_share : (at + 1) * half_share, :] = parts[at]
+
+    def early(at, carry):
+        advance_maps(FIRST + at * 7, 7, 7)
+        return carry
+
+    advance_maps(1, FIRST - 1, 0)
+    lax.fori_loop(0, (STEP_DEV - FIRST) // 7, early, 0)
     half_ref[...] = full_ref[...]
-    lax.fori_loop(STEP_DEV, STEP_DEV + STEP_DEV // 4, step, 0)
+    advance_maps(STEP_DEV, 8, 4)
 
     landed(plane_in_ref, plane_sems.at[1])
     plane_sum_ref[...] += jnp.sum(plane_in_ref[...], axis=0)
@@ -185,21 +211,49 @@
         return carry
 
     lax.fori_loop(0, depth - 1, send_line, 0)
-    lax.fori_loop(STEP_DEV + STEP_DEV // 4, PAIR * STEP_DEV, step, 0)
+
+    def late(at, carry):
+        advance_maps(STEP_DEV + 8 + at * 8, 8, 0)
+        return carry
+
+    lax.fori_loop(0, STEP_DEV // 8 - 1, late, 0)
     landed(line_in_ref, line_sems.at[1])
     sums = plane_sum_ref[level_rows(level), :] + jnp.sum(line_in_ref[...], axis=0)
     drive_ref[...] = gains_ref[...] * sums
+    filler = jnp.zeros((128 - STEP_DEV, width), F32)
+    drive_columns_ref[...] = jnp.transpose(jnp.concatenate([drive_ref[...], filler], axis=0))
+
+    lanes = lax.broadcasted_iota(jnp.int32, (width, 128), 1)
+
+    def two_steps(half, at, row, forced):
+        position = half * STEP_DEV + at
+        moved = transition_ref[:, 0:128] * row[:, 0:128]
+        for block in range(128, width, 128):
+            moved += transition_ref[:, block : block + 128] * row[:, block : block + 128]
+        if forced:
+            moved += jnp.where(lanes == at, drive_columns_ref[...], 0.0)
+        column = jnp.broadcast_to(jnp.sum(moved, axis=1, keepdims=True), (width, 128))
+        column *= factors_ref[position // 2]
+        row = jnp.concatenate(
+            [
+                jnp.sum(moved_ref[:, block : block + 128] * column, axis=0, keepdims=True)
+                for block in range(0, width, 128)
+            ],
+            axis=1,
+        )
+        if forced:
+            row += drive_ref[pl.ds(at + 1, 1), :]
+        return row * scale_ref[pl.ds(position + 1, 1), :]
 
     def forced(at, row):
-        moved = row_times(row, moved_ref) + drive_ref[pl.ds(at, 1), :]
-        return moved * scale_ref[pl.ds(side * STEP_DEV + at, 1), :]
+        return two_steps(side, 2 * at, row, True)
 
     def unforced(at, row):
-        return row_times(row, moved_ref) * scale_ref[pl.ds(at, 1), :]
-
-    shift = lax.fori_loop(0, STEP_DEV, forced, jnp.zeros_like(initial_ref))
+        return two_steps(1, 2 * at, row, False)
+
+    shift = lax.fori_loop(0, STEP_DEV // 2, forced, jnp.zeros_like(initial_ref))
     shift_ref[0:1, :] = shift
-    shift = lax.fori_loop(STEP_DEV, STEP_DEV + (1 - side) * STEP_DEV, unforced, shift)
+    shift = lax.fori_loop(0, (1 - side) * (STEP_DEV // 2), unforced, shift)
     shift_ref[1:2, :] = shift
 
     @pl.when(pair == 0)
@@ -255,12 +309,23 @@
         pltpu.make_async_copy(mid_in_ref, mid_in_ref, mid_sem).wait()
         state_ref[...] = middle + mid_in_ref[...]
 
+    between_ref[...] = jnp.zeros_like(between_ref)
+    out_ref[...] = jnp.zeros_like(out_ref)
+
     def advance(at, row):
+        between_ref[pl.ds(2 * at, 1), :] = row
         row = forced(at, row)
-        out_ref[pl.ds(at, 1), :] = row
+        out_ref[pl.ds(2 * at + 1, 1), :] = row
         return row
 
-    lax.fori_loop(0, STEP_DEV, advance, state_ref[...])
+    lax.fori_loop(0, STEP_DEV // 2, advance, state_ref[...])
+    before = between_ref[...]
+    upper, lower = split(before)
+    moved = product(upper, lower, upper_ref[...], lower_ref[...]) + before * diagonal
+    own = pl.ds(pl.multiple_of(side * STEP_DEV, STEP_DEV), STEP_DEV)
+    between = (moved + drive_ref[...]) * scale_ref[own, :]
+    parity = lax.broadcasted_iota(jnp.int32, (STEP_DEV, width), 0) % 2
+    out_ref[...] = jnp.where(parity == 0, between, out_ref[...])
 
     @pl.when(pair < n_pair - 1)
     def _():
@@ -271,7 +336,7 @@
     landed(line_in_ref, line_sems.at[0])
 
 
-def filtered(n_seg, n_grp, initial, moved, gains, counts, where_step, tiles):
+def filtered(n_seg, n_grp, initial, transition, moved, gains, counts, where_step, tiles):
     n_dev = n_seg * n_grp
     depth = 4
     n_plane = n_dev // depth
@@ -281,7 +346,7 @@
     return pl.pallas_call(
         functools.partial(filter_kernel, n_seg, n_grp),
         out_shape=jax.ShapeDtypeStruct((STEP_DEV, width), F32),
-        in_specs=[VMEM] * 6,
+        in_specs=[VMEM] * 7,
         out_specs=VMEM,
         scratch_shapes=[
             pltpu.VMEM((width, width), BF16),
@@ -289,6 +354,11 @@
             pltpu.VMEM((share, width), F32),
             pltpu.VMEM((share, width), F32),
             pltpu.VMEM((PAIR * STEP_DEV, width), F32),
+            pltpu.VMEM((PAIR * STEP_DEV, 128), F32),
+            pltpu.VMEM((width, 128), F32),
+            pltpu.VMEM((PAIR * STEP_DEV // 2, width, 128), F32),
+            pltpu.VMEM((STEP_DEV, width), F32),
+            pltpu.VMEM((width, 128), F32),
             pltpu.VMEM((STEP_DEV, width), F32),
             pltpu.VMEM((tile_count, width), BF16),
             pltpu.VMEM((tile_count, width), BF16),
@@ -314,7 +384,7 @@
         compiler_params=pltpu.CompilerParams(
             collective_id=0, has_side_effects=True, vmem_limit_bytes=48 << 20
         ),
-    )(initial, moved, gains, counts, where_step, tiles)
+    )(initial, transition, moved, gains, counts, where_step, tiles)
 
 
 def on_device(initial_state, transition, gains, tiles, tile_owner, tile_step):
@@ -329,6 +399,7 @@
         n_seg,
         n_grp,
         initial_state[None],
+        transition,
         transition.T,
         gains[None],
         counts,

time: 108 us -> 97.5 us (0.903)
  Pallas kernels: 105 us -> 93.7 us
    pallas_call x1, Pallas kernels: 105 us -> 93.7 us  [filtered(): pl.pallas_call(functools.partial(filter_kernel, n_seg, n_grp), out_shape=...]
    unnamed x8 -> x10, local copies, waits for them, and re-layouts: 2.29 us -> 2.45 us
where the time goes in v3:
time: 97.5 us; the launch traced here: 97.4 us
  Pallas kernels  93.7 us (96%)
  local copies, waits for them, and re-layouts  2.54 us (3%)
  other arithmetic  0.99 us (1%)
    pallas_call x1, Pallas kernels, filtered(): pl.pallas_call(functools.partial(filter_kernel, n_seg, n_grp), out_shape=...  93.7 us
    unnamed x10, local copies, waits for them, and re-layouts  2.45 us

profile of v3, /device:TPU:31, one launch (start us, length us, event | category | flops | bytes accessed | tf_op | source)
XLA Modules:
  0.0 97.4 jit_solution(14586023927206040042)
XLA Ops:
  0.0 0.7 bitcast_add_fusion.where_ref
  0.7 0.3 convert_reduce_fusion
  1.0 0.0 copy-start.2
  1.0 0.0 copy-start.3
  1.0 0.1 reshape.15
  1.1 0.0 copy-start
  1.1 0.0 copy-start.1
  1.1 1.7 %copy.8 = f32[512,512]{0,1:T(8,128)S(1)} copy(f32[512,512]{1,0:T(8,128)} %transition_ref.1) | data formatting | bytes 2097152 | tf_op args[1]
  2.8 0.0 copy-done.2
  2.9 0.0 copy-done.3
  2.9 0.0 copy-done
  2.9 0.1 copy-done.1
  3.0 93.7 %shard_map.64 = f32[32,512]{1,0:T(8,128)S(1)} custom-call(f32[1,512]{1,0:T(1,128)S(1)} %bitcast.12, f32[512,512]{1,0:T(8,128)S(1)} %copy-done, f32[512,512]{1,0:T(8,128)S(1)} %bitcast.8, f32[1,512]{1,0:T(1,128)S(1)} %bitcast.13, f32[16,1,128]{2,1,0:T(1,128)S(1)} %pad.4.counts_ref, s32[1,512]{1,0:T(1,128)S(1)} %bitcast_add_fusion.where_ref, ...), custom_call_target="tpu_custom_call" | custom-call | tf_op jit(solution)/shard_map/pallas_call | solution.py:346
  96.7 0.6 copy.10
  (1 shorter events, 0.0 us)
Async XLA Ops:
  1.0 1.9 %copy-start.2 = (f32[512]{0:T(512)S(1)}, f32[512]{0:T(512)}, u32[]{:S(2)}) copy-start(f32[512]{0:T(512)} %param.6) | copy-start | bytes 6148
  1.0 1.8 %copy-start.3 = (f32[512]{0:T(512)S(1)}, f32[512]{0:T(512)}, u32[]{:S(2)}) copy-start(f32[512]{0:T(512)} %param.8) | copy-start | bytes 6148
  1.1 1.8 %copy-start = (f32[512,512]{1,0:T(8,128)S(1)}, f32[512,512]{1,0:T(8,128)}, u32[]{:S(2)}) copy-start(f32[512,512]{1,0:T(8,128)} %transition_ref.1) | copy-start | bytes 3145732
  1.1 1.8 %copy-start.1 = (f32[1,512,512]{2,1,0:T(8,128)S(1)}, f32[1,512,512]{2,1,0:T(8,128)}, u32[]{:S(2)}) copy-start(f32[1,512,512]{2,1,0:T(8,128)} %param.9) | copy-start | bytes 3145732

commit v4 on v3

--- a/solution.py
+++ b/solution.py
@@ -60,6 +60,9 @@
     drive_ref,
     drive_columns_ref,
     between_ref,
+    states_ref,
+    swap_ref,
+    swap_sems,
     tile_upper_ref,
     tile_lower_ref,
     counts_in_ref,
@@ -86,17 +89,22 @@
     inner = n_seg // depth
     n_plane = inner * n_grp
     seg, grp = lax.axis_index("seg"), lax.axis_index("grp")
-    me = grp * n_seg + seg
+    level, spot = seg // inner, grp * inner + seg % inner
+
+    def turned(group, at):
+        return at + (depth - 1 - 2 * at) * (group % 2) * (1 - (group + 1) // n_grp)
+
+    def place(index):
+        group, at = index // n_seg, index % n_seg
+        return {"grp": group, "seg": turned(group, at // inner) * inner + at % inner}
+
+    own_level = turned(grp, level)
+    me = grp * n_seg + own_level * inner + seg % inner
     side = me % PAIR
     pair = me // PAIR
     mate = pair * PAIR + 1 - side
     n_pair = n_dev // PAIR
     share, width = full_ref.shape
-    level, spot = seg // inner, grp * inner + seg % inner
-
-    def place(index):
-        return {"grp": index // n_seg, "seg": index % n_seg}
-
     barrier = pltpu.get_barrier_semaphore()
 
     def greet(at, carry):
@@ -202,7 +210,7 @@
     def send_line(at, carry):
         other = (level + 1 + at) % depth
         pltpu.make_async_remote_copy(
-            src_ref=plane_sum_ref.at[level_rows(other)],
+            src_ref=plane_sum_ref.at[level_rows(turned(grp, other))],
             dst_ref=line_in_ref.at[at],
             send_sem=line_sems.at[0],
             recv_sem=line_sems.at[1],
@@ -218,7 +226,7 @@
 
     lax.fori_loop(0, STEP_DEV // 8 - 1, late, 0)
     landed(line_in_ref, line_sems.at[1])
-    sums = plane_sum_ref[level_rows(level), :] + jnp.sum(line_in_ref[...], axis=0)
+    sums = plane_sum_ref[level_rows(own_level), :] + jnp.sum(line_in_ref[...], axis=0)
     drive_ref[...] = gains_ref[...] * sums
     filler = jnp.zeros((128 - STEP_DEV, width), F32)
     drive_columns_ref[...] = jnp.transpose(jnp.concatenate([drive_ref[...], filler], axis=0))
@@ -310,12 +318,12 @@
         state_ref[...] = middle + mid_in_ref[...]
 
     between_ref[...] = jnp.zeros_like(between_ref)
-    out_ref[...] = jnp.zeros_like(out_ref)
+    states_ref[...] = jnp.zeros_like(states_ref)
 
     def advance(at, row):
         between_ref[pl.ds(2 * at, 1), :] = row
         row = forced(at, row)
-        out_ref[pl.ds(2 * at + 1, 1), :] = row
+        states_ref[pl.ds(2 * at + 1, 1), :] = row
         return row
 
     lax.fori_loop(0, STEP_DEV // 2, advance, state_ref[...])
@@ -325,7 +333,25 @@
     own = pl.ds(pl.multiple_of(side * STEP_DEV, STEP_DEV), STEP_DEV)
     between = (moved + drive_ref[...]) * scale_ref[own, :]
     parity = lax.broadcasted_iota(jnp.int32, (STEP_DEV, width), 0) % 2
-    out_ref[...] = jnp.where(parity == 0, between, out_ref[...])
+    states_ref[...] = jnp.where(parity == 0, between, states_ref[...])
+    backwards = (grp % 2) * (1 - (grp + 1) // n_grp)
+
+    @pl.when(backwards == 0)
+    def _():
+        out_ref[...] = states_ref[...]
+
+    @pl.when(backwards == 1)
+    def _():
+        swap = pltpu.make_async_remote_copy(
+            src_ref=states_ref,
+            dst_ref=swap_ref,
+            send_sem=swap_sems.at[0],
+            recv_sem=swap_sems.at[1],
+            device_id={"grp": grp, "seg": (depth - 1 - level) * inner + seg % inner},
+        )
+        swap.start()
+        swap.wait()
+        out_ref[...] = swap_ref[...]
 
     @pl.when(pair < n_pair - 1)
     def _():
@@ -360,6 +386,9 @@
             pltpu.VMEM((STEP_DEV, width), F32),
             pltpu.VMEM((width, 128), F32),
             pltpu.VMEM((STEP_DEV, width), F32),
+            pltpu.VMEM((STEP_DEV, width), F32),
+            pltpu.VMEM((STEP_DEV, width), F32),
+            pltpu.SemaphoreType.DMA((2,)),
             pltpu.VMEM((tile_count, width), BF16),
             pltpu.VMEM((tile_count, width), BF16),
             pltpu.VMEM((n_dev - 1, 1, 128), F32),

time: 97.5 us -> 95.9 us (0.984)
  Pallas kernels: 93.7 us -> 92.1 us
    pallas_call x1, Pallas kernels: 93.7 us -> 92.1 us  [filtered(): pl.pallas_call(functools.partial(filter_kernel, n_seg, n_grp), out_shape=...]
where the time goes in v4:
time: 95.9 us; the launch traced here: 95.8 us
  Pallas kernels  92.1 us (96%)
  local copies, waits for them, and re-layouts  2.54 us (3%)
  other arithmetic  0.99 us (1%)
    pallas_call x1, Pallas kernels, filtered(): pl.pallas_call(functools.partial(filter_kernel, n_seg, n_grp), out_shape=...  92.1 us
    unnamed x10, local copies, waits for them, and re-layouts  2.45 us

profile of v4, /device:TPU:31, one launch (start us, length us, event | category | flops | bytes accessed | tf_op | source)
XLA Modules:
  0.0 95.8 jit_solution(26469976990911011)
XLA Ops:
  0.0 0.7 bitcast_add_fusion.where_ref
  0.7 0.3 convert_reduce_fusion
  1.0 0.0 copy-start.2
  1.0 0.0 copy-start.3
  1.0 0.1 reshape.15
  1.1 0.0 copy-start
  1.1 0.0 copy-start.1
  1.1 1.7 %copy.8 = f32[512,512]{0,1:T(8,128)S(1)} copy(f32[512,512]{1,0:T(8,128)} %transition_ref.1) | data formatting | bytes 2097152 | tf_op args[1]
  2.8 0.0 copy-done.2
  2.9 0.0 copy-done.3
  2.9 0.0 copy-done
  2.9 0.1 copy-done.1
  3.0 92.1 %shard_map.64 = f32[32,512]{1,0:T(8,128)S(1)} custom-call(f32[1,512]{1,0:T(1,128)S(1)} %bitcast.12, f32[512,512]{1,0:T(8,128)S(1)} %copy-done, f32[512,512]{1,0:T(8,128)S(1)} %bitcast.8, f32[1,512]{1,0:T(1,128)S(1)} %bitcast.13, f32[16,1,128]{2,1,0:T(1,128)S(1)} %pad.4.counts_ref, s32[1,512]{1,0:T(1,128)S(1)} %bitcast_add_fusion.where_ref, ...), custom_call_target="tpu_custom_call" | custom-call | tf_op jit(solution)/shard_map/pallas_call | solution.py:372
  95.1 0.6 copy.10
  (1 shorter events, 0.0 us)
Async XLA Ops:
  1.0 1.9 %copy-start.2 = (f32[512]{0:T(512)S(1)}, f32[512]{0:T(512)}, u32[]{:S(2)}) copy-start(f32[512]{0:T(512)} %param.6) | copy-start | bytes 6148
  1.0 1.8 %copy-start.3 = (f32[512]{0:T(512)S(1)}, f32[512]{0:T(512)}, u32[]{:S(2)}) copy-start(f32[512]{0:T(512)} %param.8) | copy-start | bytes 6148
  1.1 1.8 %copy-start = (f32[512,512]{1,0:T(8,128)S(1)}, f32[512,512]{1,0:T(8,128)}, u32[]{:S(2)}) copy-start(f32[512,512]{1,0:T(8,128)} %transition_ref.1) | copy-start | bytes 3145732
  1.1 1.8 %copy-start.1 = (f32[1,512,512]{2,1,0:T(8,128)S(1)}, f32[1,512,512]{2,1,0:T(8,128)}, u32[]{:S(2)}) copy-start(f32[1,512,512]{2,1,0:T(8,128)} %param.9) | copy-start | bytes 3145732
